TPU v7x, 256 devices: a whole 4x4x8 slice. The times are simulated.
256 devices in a mesh: slab: 16 (over x_hi, y, core), batch: 16 (over x_lo, z).
Axes of the slice: x: 4 (x_hi: 2, x_lo: 2; x = x_hi * 2 + x_lo), y: 4, z: 8, core: 2. Of those that a mesh axis runs over, the one named last changes fastest.
Arguments:
- volumes: bfloat16 [256, 2, 16384], P('slab', None, 'batch'), may hold values from -6 to 6
- band_weights: bfloat16 [2, 1024, 32], P(None, 'slab'), may hold values from -1 to 1
- band_start: int32 [2, 1024], P(None, 'slab'), may hold values from 0 to 224
- images: bfloat16 [6144, 16384], P('batch'), may hold values from -7 to 7
- noise_precision: float32 [6144], P('batch'), may hold values from 0.005004883 to 0.050048828
- log_prior: float32 [2, 1024], P(None, 'slab'), may hold values from -4 to 4
Outputs:
- responsibilities: float32 [2, 1024, 6144], P(None, 'slab', 'batch')
- log_evidence: float32 [6144], P('batch')
- backprojection: float32 [256, 2, 16384], P('slab', None, 'batch')
All inputs are finite; a program needn't handle non-finite values.
Results may differ from a plain program's by a relative error of at most 0.0069.
Values may be sent and summed in bfloat16 or wider, within the bound.
A program may use at most 64 MiB of HBM per device.

v0:
```python
import jax
import jax.numpy as jnp
from jax import lax
from jax.sharding import PartitionSpec as P


def joined_along(pieces, dim):
    pieces = jnp.moveaxis(pieces, 0, dim)
    shape = pieces.shape
    return pieces.reshape(*shape[:dim], shape[dim] * shape[dim + 1], *shape[dim + 2 :])


def copy_for_each(x, axis):
    copies = jnp.broadcast_to(x, (lax.axis_size(axis), *x.shape))
    return lax.all_to_all(copies, axis, split_axis=0, concat_axis=0, tiled=True)


def collect(x, axis, dim):
    return joined_along(copy_for_each(x, axis), dim)


def gathered_once(x, axis):
    leaves = jax.tree.leaves(x)
    sequence = sorted(range(len(leaves)), key=lambda k: -leaves[k].size)
    width = (1, *leaves[sequence[0]].shape)[-1]
    lines = [
        jnp.pad(leaves[k].reshape(-1), (0, -leaves[k].size % width)).reshape(-1, width)
        for k in sequence
    ]
    both, at, found = (copy_for_each(jnp.concatenate(lines), axis), 0, {})
    for k, line in zip(sequence, lines):
        piece = both[:, at : at + len(line)].reshape(len(both), -1)
        found[k] = piece[:, : leaves[k].size].reshape(-1, *leaves[k].shape)
        at += len(line)
    numbers = iter(range(len(leaves)))
    return jax.tree.map(lambda _: found[next(numbers)], x)


def folded_in_pairs(pieces, combine):
    while len(jax.tree.leaves(pieces)[0]) > 1:
        pieces = jax.vmap(combine)(
            *(jax.tree.map(lambda part: part[side::2], pieces) for side in (0, 1))
        )
    return jax.tree.map(lambda part: part[0], pieces)


def joined_all(x, axis, combine):
    pieces = gathered_once(x, axis)
    return folded_in_pairs(pieces, combine)


def cut_along(x, dim, count):
    before, after = (x.shape[:dim], x.shape[dim + 1 :])
    return jnp.moveaxis(x.reshape(*before, count, -1, *after), dim, 0)


def sum_at_owner(x, axis, dim):
    pieces = cut_along(x, dim, lax.axis_size(axis))
    arrived = lax.all_to_all(pieces, axis, split_axis=0, concat_axis=0, tiled=True)
    return arrived.sum(axis=0)


def build_slice(band_weights, band_start, planes):
    offsets = planes[None, None, :] - band_start[:, :, None]
    taps = jnp.arange(band_weights.shape[2], dtype=jnp.int32)
    hits = offsets[..., None] == taps
    values = jnp.where(hits, band_weights.astype(jnp.float32)[:, :, None, :], jnp.float32(0.0))
    return jnp.sum(values, axis=-1)


def combine_scores(first, second):
    top_one, total_one = first
    top_two, total_two = second
    joined = jnp.maximum(top_one, top_two)
    return (joined, total_one * jnp.exp(top_one - joined) + total_two * jnp.exp(top_two - joined))


def local(volumes, band_weights, band_start, images, noise_precision, log_prior):
    plane_count, classes, block = volumes.shape
    all_planes = plane_count * lax.axis_size("slab")
    slice_own = build_slice(band_weights, band_start, jnp.arange(all_planes, dtype=jnp.int32))
    gathered = collect(volumes, "slab", 0)
    projection = jnp.einsum(
        "koz,zkp->okp", slice_own.astype(jnp.bfloat16), gathered, preferred_element_type=jnp.float32
    ).astype(jnp.bfloat16)
    piece = lax.all_gather(projection, "batch", axis=2, tiled=True)
    columns = images
    inner = jnp.einsum("okp,np->kon", piece, columns, preferred_element_type=jnp.float32)
    wide = piece.astype(jnp.float32)
    inner, energy = (inner, jnp.sum(wide * wide, axis=2))
    score = (
        noise_precision[None, None, :] * (inner - 0.5 * energy.T[:, :, None])
        + log_prior[:, :, None]
    )
    local_top = jnp.max(score, axis=(0, 1))
    local_total = jnp.sum(jnp.exp(score - local_top[None, None, :]), axis=(0, 1))
    top, total = joined_all((local_top, local_total), "slab", combine_scores)
    log_evidence = top + jnp.log(total)
    responsibilities = jnp.exp(score - log_evidence[None, None, :])
    weights = responsibilities.astype(jnp.bfloat16)
    columns = images
    image_sum = lax.psum_scatter(
        jnp.einsum("np,kon->pko", columns, weights, preferred_element_type=jnp.float32),
        "batch",
        scatter_dimension=0,
        tiled=True,
    )
    backprojection = sum_at_owner(
        jnp.einsum("koz,pko->zkp", slice_own, image_sum, precision=lax.Precision.HIGHEST), "slab", 0
    )
    return (responsibilities, log_evidence, backprojection)


def solution(mesh):
    in_specs = (
        P("slab", None, "batch"),
        P(None, "slab", None),
        P(None, "slab"),
        P("batch", None),
        P("batch"),
        P(None, "slab"),
    )
    out_specs = (P(None, "slab", "batch"), P("batch"), P("slab", None, "batch"))
    return jax.shard_map(local, mesh=mesh, in_specs=in_specs, out_specs=out_specs, check_vma=False)
```

profile of v0, /device:TPU:1, one launch (start us, length us, event | category | flops | bytes accessed | tf_op | source)
XLA Modules:
  0.0 288.5 jit_solution(14780554154317257893)
XLA Ops:
  7.2 0.9 copy.20
  8.0 1.1 broadcast_in_dim.18
  9.1 8.4 %all-to-all-start = ((bf16[16,16,2,1024]{3,1,2,0:T(8,128)(2,1)}), bf16[16,16,2,1024]{3,1,2,0:T(8,128)(2,1)S(1)}, u32[]{:S(2)}, u32[]{:S(2)}) async-start(bf16[16,16,2,1024]{3,1,2,0:T(8,128)(2,1)} %broadcast_in_dim.18), calls=%async_computation | async-start | bytes 2097152 | tf_op jit(solution)/shard_map/all_to_all | solution.py:15
  17.6 0.0 all-gather.2.cloned.1.call-start
  17.6 0.8 copy.19
  18.4 0.8 iota_subtract_fusion
  19.2 0.0 copy-start.3
  19.2 0.0 copy-start.4
  19.2 1.1 select_reduce_fusion
  20.3 14.3 %all-to-all-done = bf16[16,16,2,1024]{3,1,2,0:T(8,128)(2,1)S(1)} async-done(((bf16[16,16,2,1024]{3,1,2,0:T(8,128)(2,1)}), bf16[16,16,2,1024]{3,1,2,0:T(8,128)(2,1)S(1)}, u32[]{:S(2)}, u32[]{:S(2)}) %all-to-all-start) | async-done | bytes 1048608 | tf_op jit(solution)/shard_map/all_to_all | solution.py:15
  34.7 0.1 copy.21
  34.8 1.0 fusion.3
  35.8 0.0 all-gather.2.cloned.1.call-update
  35.8 0.0 reduce-scatter.2.cloned.1.call-start
  35.8 65.5 %all-gather.2.cloned.1.call-done = bf16[64,2,16384]{2,0,1:T(8,128)(2,1)} async-done(((bf16[64,2,1024]{2,0,1:T(8,128)(2,1)}), bf16[64,2,16384]{2,0,1:T(8,128)(2,1)}) %all-gather.2.cloned.1.call-update) | async-done | bytes 4194320 | tf_op jit(solution)/shard_map/all_gather | solution.py:86
  101.4 0.0 copy-start
  101.4 3.3 %multiply_reduce_fusion = f32[64,2]{0,1:T(2,128)S(1)} fusion(bf16[64,2,16384]{2,0,1:T(8,128)(2,1)} %all-gather.2.cloned.1.call-done), kind=kLoop, calls=%fused_computation.4 | loop fusion | flops 6291328 | bytes 4194816 | tf_op jit(solution)/shard_map/reduce_sum | solution.py:90
  104.7 0.0 copy-done.3
  104.7 0.0 copy-done.4
  104.7 0.1 copy-done
  104.8 8.4 %fusion.21 = (f32[384]{0:T(512)S(1)}, f32[2,64,384]{2,1,0:T(8,128)S(1)}) fusion(f32[2,64]{1,0:T(2,128)S(1)} %copy-done.4, f32[2,64]{1,0:T(2,128)S(1)} %multiply_bitcast_fusion, bf16[64,2,16384]{2,0,1:T(8,128)(2,1)S(1)} %copy-done, bf16[384,16384]{1,0:T(8,128)(2,1)} %param.9, f32[384]{0:T(512)S(1)} %copy-done.3), kind=kOutput, calls=%fused_computation.32 | convolution fusion | flops 1610808960 | bytes 16977920 | tf_op jit(solution)/shard_map/okp,np->kon/dot_general | solution.py:88
  113.2 0.1 exponential_reduce_fusion
  113.3 24.0 %all_to_all.15 = f32[16,2,384]{2,1,0:T(2,128)S(1)} all-to-all(f32[16,2,384]{2,1,0:T(2,128)S(1)} %broadcast_in_dim.19), channel_id=1, replica_groups=mesh['slab'=16,'batch'=16] {'slab'}, dimensions={0} | all-to-all | bytes 98304 | tf_op jit(solution)/shard_map/all_to_all | solution.py:15
  137.7 0.0 copy-start.2
  137.8 0.0 copy-start.1
  137.8 10.2 %convolution_bitcast_fusion = f32[16384,2,64]{0,2,1:T(8,128)} fusion(bf16[384,16384]{1,0:T(8,128)(2,1)} %param.9, f32[2,64,384]{2,1,0:T(8,128)S(1)} %subtract_exponential_fusion), kind=kOutput, calls=%fused_computation | convolution fusion | flops 1610661888 | bytes 21168128 | tf_op jit(solution)/shard_map/np,kon->pko/dot_general | solution.py:103
  148.0 0.0 copy-done.2
  148.0 0.0 copy-done.1
  148.0 0.0 reduce-scatter.2.cloned.1.call-update
  148.0 94.6 %reduce-scatter.2.cloned.1.call-done = f32[1024,2,64]{0,2,1:T(8,128)} async-done(((f32[16384,2,64]{0,2,1:T(8,128)}), f32[1024,2,64]{0,2,1:T(8,128)}) %reduce-scatter.2.cloned.1.call-update) | async-done | bytes 524304 | tf_op jit(solution)/shard_map/reduce_scatter | solution.py:102
  242.7 2.9 fusion.22
  245.5 0.2 copy.23
  245.8 35.0 %all_to_all.16 = f32[16,16,2,1024]{3,1,2,0:T(8,128)S(1)} all-to-all(f32[16,16,2,1024]{3,1,2,0:T(8,128)S(1)} %copy.23), channel_id=1, replica_groups=mesh['slab'=16,'batch'=16] {'slab'}, dimensions={0} | all-to-all | bytes 4194304 | tf_op jit(solution)/shard_map/all_to_all | solution.py:59
  280.7 0.1 reduce_sum.39
  280.9 0.8 copy.25
  (24 shorter events, 0.5 us)
Async XLA Ops:
  9.1 25.5 %all-to-all-start = ((bf16[16,16,2,1024]{3,1,2,0:T(8,128)(2,1)}), bf16[16,16,2,1024]{3,1,2,0:T(8,128)(2,1)S(1)}, u32[]{:S(2)}, u32[]{:S(2)}) async-start(bf16[16,16,2,1024]{3,1,2,0:T(8,128)(2,1)} %broadcast_in_dim.18), calls=%async_computation | async-start | bytes 2097152 | tf_op jit(solution)/shard_map/all_to_all | solution.py:15
  17.6 83.8 %all-gather.2.cloned.1.call-start = ((), (), s32[]{:S(2)}) async-start(), calls=%async_computation.4 | async-start | bytes 4456448 | tf_op jit(solution)/shard_map/all_gather | solution.py:86
  19.2 85.5 %copy-start.3 = (f32[384]{0:T(512)S(1)}, f32[384]{0:T(512)}, u32[]{:S(2)}) copy-start(f32[384]{0:T(512)} %param.10) | copy-start | bytes 4612
  19.2 85.5 %copy-start.4 = (f32[2,64]{1,0:T(2,128)S(1)}, f32[2,64]{1,0:T(2,128)}, u32[]{:S(2)}) copy-start(f32[2,64]{1,0:T(2,128)} %param.11) | copy-start | bytes 1540
  35.8 206.9 %reduce-scatter.2.cloned.1.call-start = ((), (), s32[]{:S(2)}) async-start(), calls=%async_computation.5 | async-start | bytes 8912896 | tf_op jit(solution)/shard_map/reduce_scatter | solution.py:102
  101.4 3.4 %copy-start = (bf16[64,2,16384]{2,0,1:T(8,128)(2,1)S(1)}, bf16[64,2,16384]{2,0,1:T(8,128)(2,1)}, u32[]{:S(2)}) copy-start(bf16[64,2,16384]{2,0,1:T(8,128)(2,1)} %all-gather.2.cloned.1.call-done) | copy-start | bytes 12582916
  137.7 10.3 %copy-start.2 = (f32[384]{0:T(512)}, f32[384]{0:T(512)S(1)}, u32[]{:S(2)}) copy-start(f32[384]{0:T(512)S(1)} %add_reduce_fusion) | copy-start | bytes 4612
  137.8 10.2 %copy-start.1 = (f32[2,64,384]{2,1,0:T(8,128)}, f32[2,64,384]{2,1,0:T(8,128)S(1)}, u32[]{:S(2)}) copy-start(f32[2,64,384]{2,1,0:T(8,128)S(1)} %subtract_exponential_fusion) | copy-start | bytes 589828
Sparse Core Ops, SparseCore 0:
  35.9 65.4 all-gather.1
  148.1 94.4 reduce-scatter.1
where the time goes:
time: 289 us; the launch traced here: 288 us
  waiting for transfers between devices  175 us (61%)
  blocking collectives  58.9 us (20%)
  matrix products  22.5 us (8%)
  between operations  14.2 us (5%)
  starting transfers between devices  8.51 us (3%)
  other arithmetic  5.44 us (2%)
  local copies, waits for them, and re-layouts  4.35 us (2%)
    reduce_scatter x1, waiting for transfers between devices, local(): lax.psum_scatter(jnp.einsum('np,kon->pko', columns, weights, preferred_el...  94.6 us
    all_gather x1, waiting for transfers between devices, local(): piece = lax.all_gather(projection, 'batch', axis=2, tiled=True)  65.5 us
    all_to_all x1, blocking collectives, sum_at_owner(): lax.all_to_all(pieces, axis, split_axis=0, concat_axis=0, tiled=True)  35 us
    all_to_all x1, blocking collectives, copy_for_each(): return lax.all_to_all(copies, axis, split_axis=0, concat_axis=0, tiled=True)  24 us
    all_to_all x1, waiting for transfers between devices, copy_for_each(): return lax.all_to_all(copies, axis, split_axis=0, concat_axis=0, tiled=True)  14.3 us
    dot_general x1, matrix products, local(): jnp.einsum('np,kon->pko', columns, weights, preferred_element_type=jnp.fl...  10.2 us
    all_to_all x1, starting transfers between devices, copy_for_each(): return lax.all_to_all(copies, axis, split_axis=0, concat_axis=0, tiled=True)  8.44 us
    dot_general x1, matrix products, local(): jnp.einsum('okp,np->kon', piece, columns, preferred_element_type=jnp.floa...  8.39 us
  transfers between devices with their start and end apart: 3, of which 3 were waited for; matrix products, arithmetic and copies ran while one was open for 1% of the time, Pallas kernels for 0%

commit v1 on v0

--- a/solution.py
+++ b/solution.py
@@ -83,7 +83,9 @@
     projection = jnp.einsum(
         "koz,zkp->okp", slice_own.astype(jnp.bfloat16), gathered, preferred_element_type=jnp.float32
     ).astype(jnp.bfloat16)
-    piece = lax.all_gather(projection, "batch", axis=2, tiled=True)
+    upper = jnp.stack([projection for _ in range(lax.axis_size("batch"))], 0)
+    met_up = lax.all_to_all(upper, "batch", split_axis=0, concat_axis=0)
+    piece = jnp.concatenate(met_up, 2)
     columns = images
     inner = jnp.einsum("okp,np->kon", piece, columns, preferred_element_type=jnp.float32)
     wide = piece.astype(jnp.float32)

time: 289 us -> 312 us (1.080)
  blocking collectives: 58.9 us -> 150 us
  waiting for transfers between devices: 175 us -> 110 us
    all_to_all x0 -> x1, blocking collectives: none -> 99.9 us  [local(): met_up = lax.all_to_all(upper, 'batch', split_axis=0, concat_axis=0)]
    all_gather x1 -> x0, waiting for transfers between devices: 65.5 us -> none  [local(): piece = lax.all_gather(projection, 'batch', axis=2, tiled=True)]
    all_to_all x1, blocking collectives: 24 us -> 14.7 us  [copy_for_each(): return lax.all_to_all(copies, axis, split_axis=0, concat_axis=0, tiled=True)]
  transfers between devices with their start and end apart: 3 -> 2, of which waited for: 3 -> 2; matrix products, arithmetic and copies ran while one was open for 1% -> 1% of each run, Pallas kernels for 0% -> 0%
where the time goes in v1:
time: 312 us
  blocking collectives  150 us (48%)
  waiting for transfers between devices  110 us (35%)
  matrix products  19.4 us (6%)
  between operations  14.2 us (5%)
  starting transfers between devices  8.47 us (3%)
  local copies, waits for them, and re-layouts  7.14 us (2%)
    all_to_all x1, blocking collectives, local(): met_up = lax.all_to_all(upper, 'batch', split_axis=0, concat_axis=0)  99.9 us
    reduce_scatter x1, waiting for transfers between devices, local(): lax.psum_scatter(jnp.einsum('np,kon->pko', columns, weights, preferred_el...  95.4 us
    all_to_all x1, blocking collectives, sum_at_owner(): lax.all_to_all(pieces, axis, split_axis=0, concat_axis=0, tiled=True)  35 us
    all_to_all x1, blocking collectives, copy_for_each(): return lax.all_to_all(copies, axis, split_axis=0, concat_axis=0, tiled=True)  14.7 us
    all_to_all x1, waiting for transfers between devices, copy_for_each(): return lax.all_to_all(copies, axis, split_axis=0, concat_axis=0, tiled=True)  14.4 us
    dot_general x1, matrix products, local(): jnp.einsum('np,kon->pko', columns, weights, preferred_element_type=jnp.fl...  10.2 us
    all_to_all x1, starting transfers between devices, copy_for_each(): return lax.all_to_all(copies, axis, split_axis=0, concat_axis=0, tiled=True)  8.44 us
  transfers between devices with their start and end apart: 2, of which 2 were waited for; matrix products, arithmetic and copies ran while one was open for 1% of the time, Pallas kernels for 0%

profile of v1, /device:TPU:1, one launch (start us, length us, event | category | flops | bytes accessed | tf_op | source)
XLA Modules:
  0.0 311.7 jit_solution(100258624626324401)
XLA Ops:
  7.2 0.9 copy.21
  8.0 1.1 broadcast_in_dim.18
  9.1 8.4 %all-to-all-start = ((bf16[16,16,2,1024]{3,1,2,0:T(8,128)(2,1)}), bf16[16,16,2,1024]{3,1,2,0:T(8,128)(2,1)S(1)}, u32[]{:S(2)}, u32[]{:S(2)}) async-start(bf16[16,16,2,1024]{3,1,2,0:T(8,128)(2,1)} %broadcast_in_dim.18), calls=%async_computation | async-start | bytes 2097152 | tf_op jit(solution)/shard_map/all_to_all | solution.py:15
  17.6 0.0 reduce-scatter.2.cloned.1.call-start
  17.6 0.8 copy.20
  18.4 0.8 iota_subtract_fusion
  19.2 1.1 select_reduce_fusion
  20.3 14.4 %all-to-all-done = bf16[16,16,2,1024]{3,1,2,0:T(8,128)(2,1)S(1)} async-done(((bf16[16,16,2,1024]{3,1,2,0:T(8,128)(2,1)}), bf16[16,16,2,1024]{3,1,2,0:T(8,128)(2,1)S(1)}, u32[]{:S(2)}, u32[]{:S(2)}) %all-to-all-start) | async-done | bytes 1048608 | tf_op jit(solution)/shard_map/all_to_all | solution.py:15
  34.7 0.1 copy.22
  34.8 0.3 fusion.3
  35.1 0.0 slice-start
  35.1 0.5 stack.2
  35.6 0.0 slice-start.1
  35.6 99.9 %all_to_all.20 = bf16[16,64,2,1024]{3,1,2,0:T(8,128)(2,1)S(1)} all-to-all(bf16[16,64,2,1024]{3,1,2,0:T(8,128)(2,1)S(1)} %stack.2), channel_id=1, replica_groups=mesh['slab'=16,'batch'=16] {'batch'}, dimensions={0} | all-to-all | bytes 8388608 | tf_op jit(solution)/shard_map/all_to_all | solution.py:87
  135.5 0.0 slice-start.2
  135.5 1.0 multiply_reduce_fusion
  136.5 0.0 copy-start.2
  136.5 0.0 copy-start.3
  136.5 2.4 copy.31
  138.9 0.0 slice-done
  138.9 0.0 slice-done.1
  138.9 0.0 slice-done.2
  138.9 0.0 copy-done.2
  138.9 0.0 copy-done.3
  138.9 6.0 %fusion.21 = (f32[384]{0:T(512)S(1)}, f32[2,64,384]{2,1,0:T(8,128)S(1)}) fusion(f32[2,64]{1,0:T(2,128)S(1)} %copy-done.3, f32[2,64]{1,0:T(2,128)S(1)} %multiply_bitcast_fusion, bf16[64,2,16384]{2,0,1:T(8,128)(2,1)} %bitcast.48, bf16[384,16384]{1,0:T(8,128)(2,1)S(1)} %bitcast.46, f32[384]{0:T(512)S(1)} %copy-done.2), kind=kOutput, calls=%fused_computation.32 | convolution fusion | flops 1610808960 | bytes 16977920 | tf_op jit(solution)/shard_map/okp,np->kon/dot_general | solution.py:90
  145.0 0.1 exponential_reduce_fusion
  145.1 14.7 %all_to_all.21 = f32[16,2,384]{2,1,0:T(2,128)S(1)} all-to-all(f32[16,2,384]{2,1,0:T(2,128)S(1)} %broadcast_in_dim.19), channel_id=1, replica_groups=mesh['slab'=16,'batch'=16] {'slab'}, dimensions={0} | all-to-all | bytes 98304 | tf_op jit(solution)/shard_map/all_to_all | solution.py:15
  160.2 0.0 copy-start.1
  160.2 0.0 copy-start
  160.2 10.2 %convolution_bitcast_fusion = f32[16384,2,64]{0,2,1:T(8,128)} fusion(bf16[384,16384]{1,0:T(8,128)(2,1)} %param.9, f32[2,64,384]{2,1,0:T(8,128)S(1)} %subtract_exponential_fusion), kind=kOutput, calls=%fused_computation | convolution fusion | flops 1610661888 | bytes 21168128 | tf_op jit(solution)/shard_map/np,kon->pko/dot_general | solution.py:105
  170.4 0.0 copy-done.1
  170.4 0.0 copy-done
  170.5 0.0 reduce-scatter.2.cloned.1.call-update
  170.5 95.4 %reduce-scatter.2.cloned.1.call-done = f32[1024,2,64]{0,2,1:T(8,128)} async-done(((f32[16384,2,64]{0,2,1:T(8,128)}), f32[1024,2,64]{0,2,1:T(8,128)}) %reduce-scatter.2.cloned.1.call-update) | async-done | bytes 524304 | tf_op jit(solution)/shard_map/reduce_scatter | solution.py:104
  265.9 2.9 fusion.22
  268.8 0.2 copy.25
  269.0 35.0 %all_to_all.22 = f32[16,16,2,1024]{3,1,2,0:T(8,128)S(1)} all-to-all(f32[16,16,2,1024]{3,1,2,0:T(8,128)S(1)} %copy.25), channel_id=1, replica_groups=mesh['slab'=16,'batch'=16] {'slab'}, dimensions={0} | all-to-all | bytes 4194304 | tf_op jit(solution)/shard_map/all_to_all | solution.py:59
  304.0 0.1 reduce_sum.39
  304.1 0.8 copy.27
  (25 shorter events, 0.5 us)
Async XLA Ops:
  9.1 25.5 %all-to-all-start = ((bf16[16,16,2,1024]{3,1,2,0:T(8,128)(2,1)}), bf16[16,16,2,1024]{3,1,2,0:T(8,128)(2,1)S(1)}, u32[]{:S(2)}, u32[]{:S(2)}) async-start(bf16[16,16,2,1024]{3,1,2,0:T(8,128)(2,1)} %broadcast_in_dim.18), calls=%async_computation | async-start | bytes 2097152 | tf_op jit(solution)/shard_map/all_to_all | solution.py:15
  17.6 248.3 %reduce-scatter.2.cloned.1.call-start = ((), (), s32[]{:S(2)}) async-start(), calls=%async_computation.5 | async-start | bytes 8912896 | tf_op jit(solution)/shard_map/reduce_scatter | solution.py:104
  35.1 103.8 %slice-start = ((s8[12582912]{0:T(1024)(128)(4,1)}), s8[4194304]{0:T(1024)(128)(4,1)S(1)}, s32[]{:S(2)}) async-start(s8[12582912]{0:T(1024)(128)(4,1)} %bitcast.45), calls=%async_computation.6 | async-start | bytes 8388608
  35.6 103.3 %slice-start.1 = ((s8[12582912]{0:T(1024)(128)(4,1)}), s8[4194304]{0:T(1024)(128)(4,1)S(1)}, s32[]{:S(2)}) async-start(s8[12582912]{0:T(1024)(128)(4,1)} %bitcast.45), calls=%async_computation.7 | async-start | bytes 8388608
  135.5 3.4 %slice-start.2 = ((s8[12582912]{0:T(1024)(128)(4,1)}), s8[4194304]{0:T(1024)(128)(4,1)S(1)}, s32[]{:S(2)}) async-start(s8[12582912]{0:T(1024)(128)(4,1)} %bitcast.45), calls=%async_computation.8 | async-start | bytes 8388608
  136.5 2.4 copy-start.2
  136.5 2.4 copy-start.3
  160.2 10.3 %copy-start.1 = (f32[384]{0:T(512)}, f32[384]{0:T(512)S(1)}, u32[]{:S(2)}) copy-start(f32[384]{0:T(512)S(1)} %add_reduce_fusion) | copy-start | bytes 4612
  160.2 10.2 %copy-start = (f32[2,64,384]{2,1,0:T(8,128)}, f32[2,64,384]{2,1,0:T(8,128)S(1)}, u32[]{:S(2)}) copy-start(f32[2,64,384]{2,1,0:T(8,128)S(1)} %subtract_exponential_fusion) | copy-start | bytes 589828
Sparse Core Ops, SparseCore 0:
  170.6 95.2 reduce-scatter.1
